TPU v7x, 256 devices: a whole 4x4x8 slice. The times are simulated.
256 devices in a mesh: ctx: 64 (over z, x, core), head: 4 (over y).
Axes of the slice: x: 4, y: 4, z: 8, core: 2. Of those that a mesh axis runs over, the one named last changes fastest.
Arguments:
- queries: bfloat16 [65536, 1024], P('ctx', 'head'), may hold values from -6 to 6
- keys: bfloat16 [65536, 1024], P('ctx', 'head'), may hold values from -6 to 6
- values: bfloat16 [65536, 1024], P('ctx', 'head'), may hold values from -6 to 6
- level_index: int32 [65536], P('ctx'), may hold values from 0 to 15
- level_table: float32 [16, 8, 11], P(None, 'head'), may hold values from 0.2 to 2
- head_gain: float32 [1024], P('head'), may hold values from 0.5 to 1.5
- residual: bfloat16 [65536, 1024], P(('ctx', 'head')), may hold values from -6 to 6
- w_out: bfloat16 [1024, 1024], replicated, may hold values from -0.1875 to 0.1875
- norm_gain: float32 [1024], replicated, may hold values from 0.5 to 1.5
- w_qkv: bfloat16 [1024, 3072], replicated, may hold values from -8 to 8
- windows: int32 [8], replicated, may hold values from 64 to 256, as said below
Outputs:
- hidden: bfloat16 [65536, 1024], P(('ctx', 'head'))
- attended: bfloat16 [65536, 1024], P('ctx', 'head')
Inputs may be any that keep to these rules, and one draw needn't show every extreme that they name: `windows`: each head's key window; some head's window is exactly 256 in every draw.
All inputs are finite; a program needn't handle non-finite values.
Results may differ from a plain program's by a relative error of at most 0.014.
Values may be sent and summed in bfloat16 or wider, within the bound.
No kernel may reach another device: no remote copies, remote signals or barrier semaphores. Data moves between devices by JAX's collectives and lax.ppermute only.
A program may use at most 128 MiB of HBM per device.

v0:
```python
import jax
import jax.numpy as jnp
from jax import lax
from jax.sharding import PartitionSpec as P

STRETCH = 64
WINDOW = 256
EPSILON = 1e-05
PRECISE = lax.Precision.HIGHEST


def from_behind(block, axis, distance):
    devices = range(lax.axis_size(axis))
    route = [(i - distance, i) for i in devices if i - distance in devices]
    return lax.ppermute(block, axis, route)


def bfloat(array):
    return array.astype(jnp.bfloat16)


def attend_block(
    query_block, key_block, value_block, head_windows, query_pos, key_pos, score_scale
):
    scores = (
        jnp.einsum("qhd,khd->hqk", query_block, key_block, preferred_element_type=jnp.float32)
        * score_scale
    )
    distance = query_pos[:, None] - key_pos[None, :]
    allowed = (
        (distance >= 0)[None]
        & (distance < head_windows[:, None, None])
        & (key_pos >= 0)[None, None, :]
    )
    scores = jnp.where(allowed, scores, -1e30)
    row_max = jnp.max(scores, -1, keepdims=True)
    weights = jnp.exp(scores - row_max)
    probs = bfloat(weights / jnp.sum(weights, -1, keepdims=True))
    return bfloat(
        jnp.einsum("hqk,khd->qhd", probs, value_block, preferred_element_type=jnp.float32)
    )


def windowed(query_rows, key_value, head_windows, first_pos, context_rows, score_scale):
    query_count = query_rows.shape[0]
    block_rows = min(query_count, 512)
    block_count = query_count // block_rows

    def attend_one(block_index):
        offset = block_index * block_rows
        query_block = lax.dynamic_slice_in_dim(query_rows, offset, block_rows, 0)
        pair_block = lax.dynamic_slice_in_dim(key_value, offset, context_rows + block_rows, 0)
        query_pos = first_pos + offset + jnp.arange(block_rows, dtype=jnp.int32)
        key_pos = (
            first_pos
            + offset
            - context_rows
            + jnp.arange(context_rows + block_rows, dtype=jnp.int32)
        )
        return attend_block(
            query_block,
            pair_block[:, 0],
            pair_block[:, 1],
            head_windows,
            query_pos,
            key_pos,
            score_scale,
        )

    results = lax.map(attend_one, jnp.arange(block_count, dtype=jnp.int32))
    return results.reshape((query_count,) + query_rows.shape[1:])


def per_device(
    queries,
    keys,
    values,
    level_index,
    level_table,
    head_gain,
    residual,
    w_out,
    norm_gain,
    w_qkv,
    windows,
):
    token_count = queries.shape[0]
    local_heads = level_table.shape[1]
    levels = level_table.shape[2]
    head_dim = head_gain.shape[0] // local_heads
    stretch_len = STRETCH
    stretches = token_count // stretch_len
    local_bits = stretches.bit_length() - 1
    ctx_bits = lax.axis_size("ctx").bit_length() - 1
    position = lax.axis_index("ctx")
    stretch_shape = (stretches, stretch_len, local_heads, head_dim)
    query_stretches = queries.reshape(stretch_shape)
    key_stretches = keys.reshape(stretch_shape)
    value_stretches = values.reshape(stretch_shape)
    states = jnp.einsum(
        "jchd,jche->jhde", key_stretches, value_stretches, preferred_element_type=jnp.float32
    )
    device_state = jnp.sum(states, 0).reshape(local_heads * head_dim, head_dim)
    piece = lax.all_gather(device_state[None], "ctx", axis=0, tiled=True)
    piece_rows = piece.shape[0]
    source = jnp.arange(piece_rows, dtype=jnp.int32)
    span_sizes = 2 ** jnp.arange(ctx_bits, dtype=jnp.int32)
    lower_edge = position // (2 * span_sizes) * (2 * span_sizes)
    upper_edge = position // span_sizes * span_sizes
    member = ((source[:, None] >= lower_edge[None]) & (source[:, None] < upper_edge[None])).astype(
        jnp.float32
    )
    remote = jnp.einsum("nb,nxy->bxy", member, piece, precision=PRECISE)
    level_rows = level_table.reshape(level_table.shape[0], local_heads * levels)
    onehot = (
        level_index[:, None] == jnp.arange(level_rows.shape[0], dtype=jnp.int32)[None]
    ).astype(jnp.float32)
    level_weight = jnp.dot(onehot, level_rows, precision=PRECISE).reshape(
        stretches, stretch_len, local_heads, levels
    )
    causal = (
        jnp.arange(stretch_len, dtype=jnp.int32)[:, None]
        >= jnp.arange(stretch_len, dtype=jnp.int32)[None, :]
    )
    scores = jnp.einsum(
        "jthd,jshd->jhts", query_stretches, key_stretches, preferred_element_type=jnp.float32
    )
    scores = bfloat(jnp.where(causal[None, None], scores, 0.0))
    inside = jnp.einsum(
        "jhts,jshd->jthd", scores, value_stretches, preferred_element_type=jnp.float32
    )
    running = level_weight[..., 0:1] * stretch_len ** (-0.5) * inside
    for level_bit in range(local_bits):
        block_len = 2**level_bit
        group_total = stretches // block_len
        grouped = jnp.sum(
            states.reshape(group_total, block_len, local_heads, head_dim, head_dim), 1
        )
        earlier = jnp.concatenate([jnp.zeros_like(grouped[:1]), grouped[:-1]], 0)
        odd_mask = (jnp.arange(group_total, dtype=jnp.int32) % 2).astype(jnp.float32)
        read_state = bfloat(earlier * odd_mask[:, None, None, None])
        blocked_query = query_stretches.reshape(
            group_total, block_len * stretch_len, local_heads, head_dim
        )
        part_sum = jnp.einsum(
            "mthd,mhde->mthe", blocked_query, read_state, preferred_element_type=jnp.float32
        )
        weight_now = level_weight[..., 1 + level_bit : 2 + level_bit] * (
            stretch_len * block_len
        ) ** (-0.5)
        running = running + weight_now * part_sum.reshape(stretch_shape)
    remote_read = bfloat(remote.reshape(ctx_bits, local_heads, head_dim, head_dim))
    flat_query = queries.reshape(token_count, local_heads, head_dim)
    far_terms = jnp.einsum(
        "thd,bhde->tbhe", flat_query, remote_read, preferred_element_type=jnp.float32
    )
    far_rates = jnp.array(
        [(stretch_len * 2 ** (local_bits + level_bit)) ** (-0.5) for level_bit in range(ctx_bits)],
        jnp.float32,
    )
    far_weights = (
        level_weight.reshape(token_count, local_heads, levels)[:, :, 1 + local_bits :] * far_rates
    )
    running = running.reshape(token_count, local_heads, head_dim) + jnp.einsum(
        "tbhe,thb->the", far_terms, far_weights, precision=PRECISE
    )
    mean_square = jnp.mean(running * running, -1, keepdims=True)
    heads_out = bfloat(
        running * lax.rsqrt(mean_square + EPSILON) * head_gain.reshape(local_heads, head_dim)
    )
    group_count = lax.axis_size("head")
    row_count = token_count // group_count
    sectioned = heads_out.reshape(group_count, row_count, local_heads * head_dim)
    projected = jnp.einsum(
        "grc,cd->grd",
        lax.all_to_all(sectioned, "head", split_axis=0, concat_axis=2, tiled=True),
        w_out,
        preferred_element_type=jnp.float32,
    )
    hidden = bfloat(residual.astype(jnp.float32) + projected[0])
    hidden_f = hidden.astype(jnp.float32)
    normed = bfloat(
        hidden_f * lax.rsqrt(jnp.mean(hidden_f * hidden_f, -1, keepdims=True) + EPSILON) * norm_gain
    )
    projected_qkv = bfloat(jnp.dot(normed, w_qkv, preferred_element_type=jnp.float32))
    score_scale = head_dim ** (-0.5)
    split_qkv = projected_qkv.reshape(row_count, 3, group_count, local_heads * head_dim)
    local_qkv = lax.all_to_all(split_qkv, "head", split_axis=2, concat_axis=0, tiled=True)
    local_qkv = local_qkv.reshape(token_count, 3, local_heads, head_dim)
    tail_len = min(token_count, WINDOW)
    need_count = (WINDOW - 1 + token_count - 1) // token_count
    tail_pairs = local_qkv[token_count - tail_len :, 1:3]
    before = [from_behind(tail_pairs, "ctx", 1)]
    key_value = jnp.concatenate(before + [local_qkv[:, 1:3]], 0)
    head_windows = lax.dynamic_slice_in_dim(
        windows, lax.axis_index("head") * local_heads, local_heads
    )
    first_pos = position * token_count
    result = windowed(
        local_qkv[:, 0], key_value, head_windows, first_pos, need_count * tail_len, score_scale
    )
    return (hidden, result.reshape(token_count, local_heads * head_dim))


def solution(mesh):
    in_specs = (
        P("ctx", "head"),
        P("ctx", "head"),
        P("ctx", "head"),
        P("ctx"),
        P(None, "head", None),
        P("head"),
        P(("ctx", "head"), None),
        P(),
        P(),
        P(),
        P(),
    )
    out_specs = (P(("ctx", "head"), None), P("ctx", "head"))
    return jax.shard_map(
        per_device, mesh=mesh, in_specs=in_specs, out_specs=out_specs, check_vma=False
    )
```

profile of v0, /device:TPU:32, one launch (start us, length us, event | category | flops | bytes accessed | tf_op | source)
XLA Modules:
  0.0 231.0 jit_solution(5243764467069019587)
XLA Ops:
  8.5 2.0 reshape.270
  10.6 3.6 %fusion.96 = (f32[2,128,128]{2,1,0:T(8,128)}, f32[16,2,128,128]{3,2,1,0:T(8,128)}) fusion(bf16[16,64,2,128]{3,2,1,0:T(2,128)(2,1)} %reshape.270, bf16[16,64,2,128]{3,2,1,0:T(2,128)(2,1)S(1)} %reshape.269), kind=kOutput, calls=%fused_computation.147 | convolution fusion | flops 67600384 | bytes 3276800 | tf_op jit(solution)/shard_map/jchd,jche->jhde/dot_general | solution.py:100
  19.6 3.2 %slice.68 = f32[15,2,128,128]{3,2,1,0:T(8,128)} slice(f32[16,2,128,128]{3,2,1,0:T(8,128)} %get-tuple-element.135), slice={[0:15], [0:2], [0:128], [0:128]} | slice | bytes 3932160 | tf_op jit(solution)/shard_map/slice | solution.py:139
  27.8 2.6 %copy.101 = f32[4,256,2,128]{3,1,0,2:T(8,128)} copy(f32[4,256,2,128]{1,3,2,0:T(8,128)} %convolution_bitcast_fusion.2) | data formatting | bytes 2097152 | tf_op jit(solution)/shard_map/mthd,mhde->mthe/transpose | solution.py:145
  30.4 1.7 bitcast_reduce_fusion
  33.6 2.6 %copy.106 = f32[2,512,2,128]{3,1,0,2:T(8,128)} copy(f32[2,512,2,128]{1,3,2,0:T(8,128)} %convolution_bitcast_fusion.1) | data formatting | bytes 2097152 | tf_op jit(solution)/shard_map/mthd,mhde->mthe/transpose | solution.py:145
  36.3 3.2 %fusion.36 = f32[16,64,2,128]{3,1,2,0:T(8,128)} fusion(f32[15,2,128,128]{3,2,1,0:T(8,128)} %slice.68, f32[16]{0:T(128)S(1)} %fusion.84, f32[16,64,2]{1,2,0:T(2,128)S(1)} %copy.90, bf16[16,64,2,128]{3,2,1,0:T(2,128)(2,1)} %reshape.268), kind=kOutput, calls=%fused_computation.54 | convolution fusion | flops 68419584 | bytes 3547200 | tf_op jit(solution)/shard_map/mthd,mhde->mthe/dot_general | solution.py:145
  39.5 4.6 %fusion.35 = f32[16,64,2,128]{3,1,2,0:T(8,128)} fusion(f32[16,64,2,128]{3,1,2,0:T(8,128)} %fusion.36, f32[16,64,2,128]{3,1,0,2:T(8,128)} %bitcast.120, f32[16,64,2,128]{3,1,0,2:T(8,128)} %bitcast.119, f32[16,64,2,128]{3,1,0,2:T(8,128)} %bitcast.118, f32[16,64,2]{1,2,0:T(2,128)S(1)} %copy.103, f32[16,64,2]{1,2,0:T(2,128)S(1)} %copy.98, ...), kind=kOutput, calls=%fused_computation.52 | convolution fusion | flops 69468160 | bytes 6852608 | tf_op jit(solution)/shard_map/jhts,jshd->jthd/dot_general | solution.py:129
  45.7 53.9 %all-gather.2.cloned.1.call-done = f32[64,256,128]{2,1,0:T(8,128)} async-done(((f32[1,256,128]{2,1,0:T(8,128)}), f32[64,256,128]{2,1,0:T(8,128)}) %all-gather.2.cloned.1.call-update) | async-done | bytes 8388624 | tf_op jit(solution)/shard_map/all_gather | solution.py:104
  99.5 10.7 %fusion.39 = bf16[6,256,128]{2,0,1:T(8,128)(2,1)S(1)} fusion(f32[64,256,128]{2,1,0:T(8,128)} %all-gather.2.cloned.1.call-done, s32[6]{0:T(128)S(1)} %get-tuple-element.138, s32[6]{0:T(128)S(1)} %get-tuple-element.139), kind=kOutput, calls=%fused_computation.61 | convolution fusion | flops 151192704 | bytes 8781872 | tf_op jit(solution)/shard_map/nb,nxy->bxy/dot_general | solution.py:113
  110.2 2.0 fusion.30
  112.2 2.6 %copy.129 = f32[1024,2,128]{2,0,1:T(8,128)} copy(f32[1024,2,128]{0,2,1:T(8,128)} %fusion.30) | data formatting | bytes 2097152 | tf_op jit(solution)/shard_map/tbhe,thb->the/dot_general | solution.py:164
  114.9 1.7 multiply_reduce_fusion
  117.9 14.0 %all_to_all.30 = bf16[4,256,256]{2,1,0:T(8,128)(2,1)S(1)} all-to-all(bf16[4,256,256]{2,1,0:T(8,128)(2,1)S(1)} %reshape.279), channel_id=1, replica_groups=mesh['ctx'=64,'head'=4] {'head'}, dimensions={0} | all-to-all | bytes 1048576 | tf_op jit(solution)/shard_map/all_to_all | solution.py:176
  132.0 1.9 fusion.42
  134.7 5.8 %convolution_convert_fusion = bf16[256,3072]{1,0:T(8,128)(2,1)} fusion(bf16[1024,3072]{1,0:T(8,128)(2,1)} %param.23, bf16[256,1024]{1,0:T(8,128)(2,1)S(1)} %get-tuple-element.137, f32[1024]{0:T(1024)S(1)} %copy-done.15, f32[256]{0:T(256)S(1)} %add_rsqrt_fusion.1), kind=kOutput, calls=%fused_computation.38 | convolution fusion | flops 1612447744 | bytes 8393728 | tf_op jit(solution)/shard_map/dot_general | solution.py:185
  140.6 4.2 %reshape.281 = bf16[256,3,4,256]{3,2,1,0:T(4,128)(2,1)} reshape(bf16[256,3072]{1,0:T(8,128)(2,1)} %convolution_convert_fusion) | data formatting | bytes 3145728 | tf_op jit(solution)/shard_map/reshape | solution.py:187
  144.8 1.6 copy.114
  146.4 22.7 %all_to_all.31 = bf16[256,3,4,256]{3,0,1,2:T(8,128)(2,1)S(1)} all-to-all(bf16[256,3,4,256]{3,0,1,2:T(8,128)(2,1)S(1)} %copy.114), channel_id=1, replica_groups=mesh['ctx'=64,'head'=4] {'head'}, dimensions={2} | all-to-all | bytes 3145728 | tf_op jit(solution)/shard_map/all_to_all | solution.py:188
  170.4 3.5 %reshape.282 = bf16[1024,3,2,128]{3,2,0,1:T(2,128)(2,1)} reshape(bf16[4,256,3,1,256]{4,1,0,2,3:T(8,128)(2,1)} %copy.115) | data formatting | bytes 3145728 | tf_op jit(solution)/shard_map/reshape | solution.py:189
  173.9 1.9 slice.76
  175.8 2.1 collective-permute-start
  180.6 5.3 %collective-permute-done = bf16[256,2,2,128]{3,2,0,1:T(2,128)(2,1)S(1)} collective-permute-done((bf16[256,2,2,128]{3,2,0,1:T(2,128)(2,1)}, bf16[256,2,2,128]{3,2,0,1:T(2,128)(2,1)S(1)}, u32[]{:S(2)}, u32[]{:S(2)}) %collective-permute-start) | collective-permute-done | bytes 262176 | tf_op jit(solution)/shard_map/ppermute | solution.py:15
  185.8 5.2 %pad_maximum_fusion = bf16[1280,2,2,128]{3,2,0,1:T(2,128)(2,1)} fusion(bf16[1024,2,2,128]{3,2,0,1:T(2,128)(2,1)S(1)} %slice-done, bf16[256,2,2,128]{3,2,0,1:T(2,128)(2,1)S(1)} %collective-permute-done), kind=kLoop, calls=%fused_computation.58 | loop fusion | flops 655360 | bytes 2621440 | tf_op jit(solution)/shard_map/concatenate | solution.py:194
  191.1 31.2 %while.12 = (s32[]{:T(128)}, bf16[2,512,2,128]{3,2,1,0:T(2,128)(2,1)}, s32[2]{0:T(128)S(1)}, bf16[1280,2,2,128]{3,2,0,1:T(2,128)(2,1)}, s32[]{:T(128)}, /*index=...) while((s32[]{:T(128)}, ...), condition=%wide.region_9.10_spmd, body=%wide.region_6.9_spmd.sunk | while | flops 617092352 | bytes 11036708 | solution.py:70
  192.2 1.7 constant_dynamic-slice_fusion.5
  196.8 3.0 %fusion.107 = f32[2,512]{1,0:T(2,128)S(1)} fusion(s32[512,768]{1,0:T(8,128)} %broadcast_subtract_fusion.2, s32[2]{0:T(128)S(1)} %get-tuple-element.220, pred[768]{0:T(1024)(128)(4,1)S(1)} %broadcast_compare_fusion.4, pred[512,768]{1,0:T(8,128)(4,1)S(1)} %broadcast_compare_fusion.5, bf16[768,1,2,128]{3,2,0,1:T(2,128)(2,1)S(1)} %get-tuple-element.185, ...), kind=kOutput, calls=%fused_computation.146.clone.1 | convolution fusion | flops 206832384 | bytes 2626312 | tf_op jit(solution)/shard_map/while/body/eval_jaxpr/sub | solution.py:37
  199.8 4.9 %fusion.108 = bf16[1,512,2,128]{1,3,2,0:T(8,128)(2,1)} fusion(f32[2,512]{1,0:T(2,128)S(1)} %fusion.107, bf16[768,1,2,128]{3,2,0,1:T(2,128)(2,1)S(1)} %get-tuple-element.186, s32[512,768]{1,0:T(8,128)} %broadcast_subtract_fusion.2, s32[2]{0:T(128)S(1)} %get-tuple-element.220, pred[768]{0:T(1024)(128)(4,1)S(1)} %broadcast_compare_fusion.4, ...), kind=kOutput, calls=%fused_computation.13.clone.1 | convolution fusion | flops 409077504 | bytes 3281672 | tf_op jit(solution)/shard_map/while/body/eval_jaxpr/hqk,khd->qhd/dot_general | solution.py:40
  207.8 1.7 constant_dynamic-slice_fusion.5
  212.3 3.0 %fusion.107 = f32[2,512]{1,0:T(2,128)S(1)} fusion(s32[512,768]{1,0:T(8,128)} %broadcast_subtract_fusion.2, s32[2]{0:T(128)S(1)} %get-tuple-element.220, pred[768]{0:T(1024)(128)(4,1)S(1)} %broadcast_compare_fusion.4, pred[512,768]{1,0:T(8,128)(4,1)S(1)} %broadcast_compare_fusion.5, bf16[768,1,2,128]{3,2,0,1:T(2,128)(2,1)S(1)} %get-tuple-element.185, ...), kind=kOutput, calls=%fused_computation.146.clone.1 | convolution fusion | flops 206832384 | bytes 2626312 | tf_op jit(solution)/shard_map/while/body/eval_jaxpr/sub | solution.py:37
  215.4 4.9 %fusion.108 = bf16[1,512,2,128]{1,3,2,0:T(8,128)(2,1)} fusion(f32[2,512]{1,0:T(2,128)S(1)} %fusion.107, bf16[768,1,2,128]{3,2,0,1:T(2,128)(2,1)S(1)} %get-tuple-element.186, s32[512,768]{1,0:T(8,128)} %broadcast_subtract_fusion.2, s32[2]{0:T(128)S(1)} %get-tuple-element.220, pred[768]{0:T(1024)(128)(4,1)S(1)} %broadcast_compare_fusion.4, ...), kind=kOutput, calls=%fused_computation.13.clone.1 | convolution fusion | flops 409077504 | bytes 3281672 | tf_op jit(solution)/shard_map/while/body/eval_jaxpr/hqk,khd->qhd/dot_general | solution.py:40
  222.3 1.9 copy.207
  (101 shorter events, 31.6 us)
Async XLA Ops:
  7.2 124.9 %copy-start = (bf16[1024,1024]{1,0:T(8,128)(2,1)S(1)}, bf16[1024,1024]{1,0:T(8,128)(2,1)}, u32[]{:S(2)}) copy-start(bf16[1024,1024]{1,0:T(8,128)(2,1)} %param.21) | copy-start | bytes 6291460
  7.2 92.4 %all-gather.2.cloned.1.call-start = ((), (), s32[]{:S(2)}) async-start(), calls=%async_computation.2 | async-start | bytes 8519680 | tf_op jit(solution)/shard_map/all_gather | solution.py:104
  8.5 5.6 %copy-start.2 = (bf16[1024,256]{1,0:T(8,128)(2,1)S(1)}, bf16[1024,256]{1,0:T(8,128)(2,1)}, u32[]{:S(2)}) copy-start(bf16[1024,256]{1,0:T(8,128)(2,1)} %param.14) | copy-start | bytes 1572868
  14.2 3.7 %copy-start.11 = (f32[16,2,11]{0,1,2:T(2,128)S(1)}, f32[16,2,11]{0,1,2:T(2,128)}, u32[]{:S(2)}) copy-start(f32[16,2,11]{0,1,2:T(2,128)} %param.18) | copy-start | bytes 4228
  14.2 3.9 %copy-start.14 = (s32[1024]{0:T(1024)S(1)}, s32[1024]{0:T(1024)}, u32[]{:S(2)}) copy-start(s32[1024]{0:T(1024)} %param.17) | copy-start | bytes 12292
  19.6 3.2 %copy-start.1 = (f32[16,2,128,128]{3,2,1,0:T(8,128)S(1)}, f32[16,2,128,128]{3,2,1,0:T(8,128)}, u32[]{:S(2)}) copy-start(f32[16,2,128,128]{3,2,1,0:T(8,128)} %get-tuple-element.135) | copy-start | bytes 6291460
  22.8 1.0 copy-start.8
  25.4 1.0 copy-start.6
  27.8 4.4 %copy-start.7 = (bf16[2,512,2,128]{3,2,1,0:T(2,128)(2,1)S(1)}, bf16[2,512,2,128]{3,2,1,0:T(2,128)(2,1)}, u32[]{:S(2)}) copy-start(bf16[2,512,2,128]{3,2,1,0:T(2,128)(2,1)} %reshape_reshape.17) | copy-start | bytes 1572868
  36.2 3.3 %copy-start.5 = (bf16[16,64,2,128]{3,2,1,0:T(2,128)(2,1)S(1)}, bf16[16,64,2,128]{3,2,1,0:T(2,128)(2,1)}, u32[]{:S(2)}) copy-start(bf16[16,64,2,128]{3,2,1,0:T(2,128)(2,1)} %reshape.270) | copy-start | bytes 1572868
  44.1 1.5 copy-start.13
  99.5 10.7 %copy-start.9 = (bf16[1024,2,128]{2,1,0:T(2,128)(2,1)S(1)}, bf16[1024,2,128]{2,1,0:T(2,128)(2,1)}, u32[]{:S(2)}) copy-start(bf16[1024,2,128]{2,1,0:T(2,128)(2,1)} %reshape.278) | copy-start | bytes 1572868
  112.2 4.3 %copy-start.12 = (f32[256]{0:T(256)S(1)}, f32[256]{0:T(256)}, u32[]{:S(2)}) copy-start(f32[256]{0:T(256)} %param.19) | copy-start | bytes 3076
  114.8 1.7 copy-start.3
  132.0 2.7 %copy-start.15 = (f32[1024]{0:T(1024)S(1)}, f32[1024]{0:T(1024)}, u32[]{:S(2)}) copy-start(f32[1024]{0:T(1024)} %param.22) | copy-start | bytes 12292
  133.9 0.8 copy-start.10
  170.4 7.6 %copy-start.16 = (s32[8]{0:T(128)S(1)}, s32[8]{0:T(128)}, u32[]{:S(2)}) copy-start(s32[8]{0:T(128)} %param.24) | copy-start | bytes 100
  173.9 11.9 %slice-start = ((bf16[1024,3,2,128]{3,2,0,1:T(2,128)(2,1)}), bf16[1024,2,2,128]{3,2,0,1:T(2,128)(2,1)S(1)}, s32[]{:S(2)}) async-start(bf16[1024,3,2,128]{3,2,0,1:T(2,128)(2,1)} %reshape.282), calls=%async_computation.3 | async-start | bytes 2097152 | tf_op jit(solution)/shard_map/slice | solution.py:194
  175.8 10.0 %collective-permute-start = (bf16[256,2,2,128]{3,2,0,1:T(2,128)(2,1)}, bf16[256,2,2,128]{3,2,0,1:T(2,128)(2,1)S(1)}, u32[]{:S(2)}, u32[]{:S(2)}) collective-permute-start(bf16[256,2,2,128]{3,2,0,1:T(2,128)(2,1)} %slice.76), channel_id=1, source_target_pairs={{0,4},{4,8},{8,12},{12,16},{16,20},{20,24},{24,28},{28,32},{32,36}... | collective-permute-start | bytes 786440 | tf_op jit(solution)/shard_map/ppermute | solution.py:15
  178.0 1.4 copy-start.4
Sparse Core Ops, SparseCore 0:
  14.3 85.1 all-gather.1
where the time goes:
time: 232 us; the launch traced here: 231 us
  waiting for transfers between devices  59.2 us (26%)
  local copies, waits for them, and re-layouts  53.3 us (23%)
  matrix products  51.2 us (22%)
  blocking collectives  36.7 us (16%)
  between operations  14.4 us (6%)
  other arithmetic  12.9 us (6%)
    all_gather x1, waiting for transfers between devices, per_device(): piece = lax.all_gather(device_state[None], 'ctx', axis=0, tiled=True)  53.9 us
    all_to_all x1, blocking collectives, per_device(): lax.all_to_all(split_qkv, 'head', split_axis=2, concat_axis=0, tiled=True)  22.7 us
    all_to_all x1, blocking collectives, per_device(): lax.all_to_all(sectioned, 'head', split_axis=0, concat_axis=2, tiled=True)  14 us
    dot_general x1, matrix products, per_device(): remote = jnp.einsum('nb,nxy->bxy', member, piece, precision=PRECISE)  10.7 us
    dot_general x2, matrix products, attend_block(): jnp.einsum('hqk,khd->qhd', probs, value_block, preferred_element_type=jnp...  9.71 us
    transpose x3, local copies, waits for them, and re-layouts, per_device(): jnp.einsum('mthd,mhde->mthe', blocked_query, read_state, preferred_elemen...  6.39 us
    dot_general x4, matrix products, per_device(): jnp.einsum('mthd,mhde->mthe', blocked_query, read_state, preferred_elemen...  6.39 us
    sub x2, matrix products, attend_block(): weights = jnp.exp(scores - row_max)  6.09 us
  transfers between devices with their start and end apart: 2, of which 2 were waited for; matrix products, arithmetic and copies ran while one was open for 13% of the time, Pallas kernels for 0%

commit v1 on v0

--- a/solution.py
+++ b/solution.py
@@ -2,6 +2,7 @@
 import jax.numpy as jnp
 from jax import lax
 from jax.sharding import PartitionSpec as P
+from jax.lax import all_to_all, axis_size
 
 STRETCH = 64
 WINDOW = 256
@@ -101,7 +102,10 @@
         "jchd,jche->jhde", key_stretches, value_stretches, preferred_element_type=jnp.float32
     )
     device_state = jnp.sum(states, 0).reshape(local_heads * head_dim, head_dim)
-    piece = lax.all_gather(device_state[None], "ctx", axis=0, tiled=True)
+    s0 = device_state[None]
+    v_next = jnp.stack([s0 for _ in range(axis_size("ctx"))], axis=0)
+    n_now = all_to_all(v_next, axis_name="ctx", split_axis=0, concat_axis=0)
+    piece = jnp.concatenate(n_now, axis=0)
     piece_rows = piece.shape[0]
     source = jnp.arange(piece_rows, dtype=jnp.int32)
     span_sizes = 2 ** jnp.arange(ctx_bits, dtype=jnp.int32)

time: 232 us -> 324 us (1.40)
  waiting for transfers between devices: 59.2 us -> 160 us
  between operations: 14.4 us -> 1.06 us
  starting transfers between devices: 2.17 us -> 14 us
  matrix products: 51.2 us -> 41.1 us
  local copies, waits for them, and re-layouts: 53.3 us -> 60 us
    all_to_all x0 -> x1, waiting for transfers between devices: none -> 155 us  [per_device(): n_now = all_to_all(v_next, axis_name='ctx', split_axis=0, concat_axis=0)]
    all_gather x1 -> x0, waiting for transfers between devices: 53.9 us -> none  [per_device(): piece = lax.all_gather(device_state[None], 'ctx', axis=0, tiled=True)]
    all_to_all x0 -> x1, starting transfers between devices: none -> 12.1 us  [per_device(): n_now = all_to_all(v_next, axis_name='ctx', split_axis=0, concat_axis=0)]
    dot_general x0 -> x1, local copies, waits for them, and re-layouts: none -> 8.24 us  [per_device(): remote = jnp.einsum('nb,nxy->bxy', member, piece, precision=PRECISE)]
    dot_general x1, matrix products: 10.7 us -> 3.14 us  [per_device(): remote = jnp.einsum('nb,nxy->bxy', member, piece, precision=PRECISE)]
    another operation x0 -> x1, local copies, waits for them, and re-layouts: none -> 4.22 us  [per_device(): v_next = jnp.stack([s0 for _ in range(axis_size('ctx'))], axis=0)]
  transfers between devices with their start and end apart: 2 -> 2, of which waited for: 2 -> 2; matrix products, arithmetic and copies ran while one was open for 13% -> 10% of each run, Pallas kernels for 0% -> 0%
where the time goes in v1:
time: 324 us; the launch traced here: 323 us
  waiting for transfers between devices  160 us (49%)
  local copies, waits for them, and re-layouts  60 us (19%)
  matrix products  41.1 us (13%)
  blocking collectives  35.6 us (11%)
  starting transfers between devices  14 us (4%)
  other arithmetic  9.75 us (3%)
    all_to_all x1, waiting for transfers between devices, per_device(): n_now = all_to_all(v_next, axis_name='ctx', split_axis=0, concat_axis=0)  155 us
    all_to_all x1, blocking collectives, per_device(): lax.all_to_all(split_qkv, 'head', split_axis=2, concat_axis=0, tiled=True)  22.1 us
    all_to_all x1, blocking collectives, per_device(): lax.all_to_all(sectioned, 'head', split_axis=0, concat_axis=2, tiled=True)  13.5 us
    all_to_all x1, starting transfers between devices, per_device(): n_now = all_to_all(v_next, axis_name='ctx', split_axis=0, concat_axis=0)  12.1 us
    dot_general x2, matrix products, attend_block(): jnp.einsum('hqk,khd->qhd', probs, value_block, preferred_element_type=jnp...  9.26 us
    dot_general x1, local copies, waits for them, and re-layouts, per_device(): remote = jnp.einsum('nb,nxy->bxy', member, piece, precision=PRECISE)  8.24 us
    dot_general x4, matrix products, per_device(): jnp.einsum('mthd,mhde->mthe', blocked_query, read_state, preferred_elemen...  6.53 us
  transfers between devices with their start and end apart: 2, of which 2 were waited for; matrix products, arithmetic and copies ran while one was open for 10% of the time, Pallas kernels for 0%

profile of v1, /device:TPU:32, one launch (start us, length us, event | category | flops | bytes accessed | tf_op | source)
XLA Modules:
  0.0 323.2 jit_solution(17230935746629678055)
XLA Ops:
  3.1 1.9 fusion.91
  5.0 4.2 %stack.3 = f32[64,1,256,128]{3,2,1,0:T(8,128)} broadcast(f32[256,128]{1,0:T(8,128)S(1)} %bitcast.130), dimensions={2,3} | broadcast | bytes 8519680 | tf_op jit(solution)/shard_map/stack | solution.py:106
  9.2 12.1 %all-to-all-start = ((f32[64,1,256,128]{3,2,1,0:T(8,128)}), f32[64,1,256,128]{3,2,1,0:T(8,128)}, u32[]{:S(2)}, u32[]{:S(2)}) async-start(f32[64,1,256,128]{3,2,1,0:T(8,128)} %stack.3), calls=%async_computation | async-start | bytes 16777216 | tf_op jit(solution)/shard_map/all_to_all | solution.py:107
  26.7 3.2 slice.68
  34.9 2.6 copy.101
  37.5 1.7 bitcast_reduce_fusion
  40.7 2.6 copy.106
  43.3 3.3 %fusion.34 = f32[16,64,2,128]{3,1,2,0:T(8,128)} fusion(f32[15,2,128,128]{3,2,1,0:T(8,128)} %slice.68, f32[16]{0:T(128)S(1)} %fusion.79, f32[16,64,2]{1,2,0:T(2,128)S(1)} %copy.90, bf16[16,64,2,128]{3,2,1,0:T(2,128)(2,1)} %reshape.275), kind=kOutput, calls=%fused_computation.52 | convolution fusion | flops 68419584 | bytes 3547200 | tf_op jit(solution)/shard_map/mthd,mhde->mthe/dot_general | solution.py:149
  46.6 4.7 %fusion.33 = f32[16,64,2,128]{3,1,2,0:T(8,128)} fusion(f32[16,64,2,128]{3,1,2,0:T(8,128)} %fusion.34, f32[16,64,2,128]{3,1,0,2:T(8,128)} %bitcast.127, f32[16,64,2,128]{3,1,0,2:T(8,128)} %bitcast.126, f32[16,64,2,128]{3,1,0,2:T(8,128)} %bitcast.125, f32[16,64,2]{1,2,0:T(2,128)S(1)} %copy.103, f32[16,64,2]{1,2,0:T(2,128)S(1)} %copy.98, ...), kind=kOutput, calls=%fused_computation.50 | convolution fusion | flops 69468160 | bytes 6852608 | tf_op jit(solution)/shard_map/jhts,jshd->jthd/dot_general | solution.py:133
  52.8 154.5 %all-to-all-done = f32[64,1,256,128]{3,2,1,0:T(8,128)} async-done(((f32[64,1,256,128]{3,2,1,0:T(8,128)}), f32[64,1,256,128]{3,2,1,0:T(8,128)}, u32[]{:S(2)}, u32[]{:S(2)}) %all-to-all-start) | async-done | bytes 8388640 | tf_op jit(solution)/shard_map/all_to_all | solution.py:107
  207.3 8.2 %copy.109 = f32[256,128,64]{1,2,0:T(8,128)S(1)} copy(f32[256,128,64]{1,0,2:T(8,128)} %bitcast.27) | data formatting | bytes 16777216 | tf_op jit(solution)/shard_map/nb,nxy->bxy/dot_general | solution.py:117
  215.6 3.1 convolution_convert_fusion.1
  218.7 2.0 fusion.28
  220.8 2.6 copy.130
  223.4 1.7 multiply_reduce_fusion
  226.4 13.5 %all_to_all.35 = bf16[4,256,256]{2,1,0:T(8,128)(2,1)S(1)} all-to-all(bf16[4,256,256]{2,1,0:T(8,128)(2,1)S(1)} %reshape.287), channel_id=1, replica_groups=mesh['ctx'=64,'head'=4] {'head'}, dimensions={0} | all-to-all | bytes 1048576 | tf_op jit(solution)/shard_map/all_to_all | solution.py:180
  240.2 1.9 fusion.37
  242.9 5.8 %convolution_convert_fusion = bf16[256,3072]{1,0:T(8,128)(2,1)} fusion(bf16[1024,3072]{1,0:T(8,128)(2,1)} %param.23, bf16[256,1024]{1,0:T(8,128)(2,1)S(1)} %get-tuple-element.137, f32[1024]{0:T(1024)S(1)} %copy-done.16, f32[256]{0:T(256)S(1)} %add_rsqrt_fusion.1), kind=kOutput, calls=%fused_computation.36 | convolution fusion | flops 1612447744 | bytes 8393728 | tf_op jit(solution)/shard_map/dot_general | solution.py:189
  248.7 3.2 reshape.289
  252.2 22.1 %all_to_all.36 = bf16[256,3,4,256]{3,0,1,2:T(8,128)(2,1)S(1)} all-to-all(bf16[256,3,4,256]{3,0,1,2:T(8,128)(2,1)S(1)} %copy.114), channel_id=1, replica_groups=mesh['ctx'=64,'head'=4] {'head'}, dimensions={2} | all-to-all | bytes 3145728 | tf_op jit(solution)/shard_map/all_to_all | solution.py:192
  275.5 2.4 reshape.290
  278.1 1.9 collective-permute-start
  282.0 5.9 %collective-permute-done = bf16[256,2,2,128]{3,2,0,1:T(2,128)(2,1)S(1)} collective-permute-done((bf16[256,2,2,128]{3,2,0,1:T(2,128)(2,1)S(1)}, bf16[256,2,2,128]{3,2,0,1:T(2,128)(2,1)S(1)}, u32[]{:S(2)}, u32[]{:S(2)}) %collective-permute-start) | collective-permute-done | bytes 262176 | tf_op jit(solution)/shard_map/ppermute | solution.py:16
  287.9 4.4 %pad_maximum_fusion = bf16[1280,2,2,128]{3,2,0,1:T(2,128)(2,1)S(1)} fusion(bf16[1024,2,2,128]{3,2,0,1:T(2,128)(2,1)S(1)} %slice.77, bf16[256,2,2,128]{3,2,0,1:T(2,128)(2,1)S(1)} %collective-permute-done), kind=kLoop, calls=%fused_computation.56 | loop fusion | flops 655360 | bytes 2621440 | tf_op jit(solution)/shard_map/concatenate | solution.py:198
  292.3 28.8 %while.12 = (s32[]{:T(128)}, bf16[2,512,2,128]{3,2,1,0:T(2,128)(2,1)}, s32[2]{0:T(128)S(1)}, bf16[1280,2,2,128]{3,2,0,1:T(2,128)(2,1)S(1)}, s32[]{:T(128)}, /*in...) while((s32[]{:T(128)}, ...), condition=%wide.region_9.10_spmd, body=%wide.region_6.9_spmd.sunk | while | flops 617092352 | bytes 11036708 | solution.py:71
  295.0 1.8 constant_dynamic-slice_fusion.6
  297.4 2.7 fusion.103
  300.1 4.6 %fusion.104 = bf16[1,512,2,128]{1,3,2,0:T(8,128)(2,1)} fusion(f32[2,512]{1,0:T(2,128)S(1)} %fusion.103, bf16[768,1,2,128]{3,2,0,1:T(2,128)(2,1)} %get-tuple-element.186, s32[512,768]{1,0:T(8,128)S(1)} %broadcast_subtract_fusion.2, s32[2]{0:T(128)S(1)} %get-tuple-element.220, pred[768]{0:T(1024)(128)(4,1)S(1)} %broadcast_compare_fusion.4, ...), kind=kOutput, calls=%fused_computation.13.clone.1 | convolution fusion | flops 409077504 | bytes 3281672 | tf_op jit(solution)/shard_map/while/body/eval_jaxpr/hqk,khd->qhd/dot_general | solution.py:41
  309.4 1.8 constant_dynamic-slice_fusion.6
  311.8 2.7 fusion.103
  314.5 4.6 %fusion.104 = bf16[1,512,2,128]{1,3,2,0:T(8,128)(2,1)} fusion(f32[2,512]{1,0:T(2,128)S(1)} %fusion.103, bf16[768,1,2,128]{3,2,0,1:T(2,128)(2,1)} %get-tuple-element.186, s32[512,768]{1,0:T(8,128)S(1)} %broadcast_subtract_fusion.2, s32[2]{0:T(128)S(1)} %get-tuple-element.220, pred[768]{0:T(1024)(128)(4,1)S(1)} %broadcast_compare_fusion.4, ...), kind=kOutput, calls=%fused_computation.13.clone.1 | convolution fusion | flops 409077504 | bytes 3281672 | tf_op jit(solution)/shard_map/while/body/eval_jaxpr/hqk,khd->qhd/dot_general | solution.py:41
  321.2 2.1 copy.204
  (103 shorter events, 30.8 us)
Async XLA Ops:
  0.6 239.5 %copy-start = (bf16[1024,1024]{1,0:T(8,128)(2,1)S(1)}, bf16[1024,1024]{1,0:T(8,128)(2,1)}, u32[]{:S(2)}) copy-start(bf16[1024,1024]{1,0:T(8,128)(2,1)} %param.21) | copy-start | bytes 6291460
  3.1 1.9 copy-start.5
  9.2 12.1 %copy-start.3 = (bf16[1024,256]{1,0:T(8,128)(2,1)S(1)}, bf16[1024,256]{1,0:T(8,128)(2,1)}, u32[]{:S(2)}) copy-start(bf16[1024,256]{1,0:T(8,128)(2,1)} %param.14) | copy-start | bytes 1572868
  9.2 198.1 %all-to-all-start = ((f32[64,1,256,128]{3,2,1,0:T(8,128)}), f32[64,1,256,128]{3,2,1,0:T(8,128)}, u32[]{:S(2)}, u32[]{:S(2)}) async-start(f32[64,1,256,128]{3,2,1,0:T(8,128)} %stack.3), calls=%async_computation | async-start | bytes 16777216 | tf_op jit(solution)/shard_map/all_to_all | solution.py:107
  21.3 3.7 %copy-start.12 = (f32[16,2,11]{0,1,2:T(2,128)S(1)}, f32[16,2,11]{0,1,2:T(2,128)}, u32[]{:S(2)}) copy-start(f32[16,2,11]{0,1,2:T(2,128)} %param.18) | copy-start | bytes 4228
  21.3 3.8 %copy-start.15 = (s32[1024]{0:T(1024)S(1)}, s32[1024]{0:T(1024)}, u32[]{:S(2)}) copy-start(s32[1024]{0:T(1024)} %param.17) | copy-start | bytes 12292
  26.7 3.2 copy-start.2
  29.9 1.0 copy-start.9
  32.4 1.0 copy-start.7
  34.9 4.4 %copy-start.8 = (bf16[2,512,2,128]{3,2,1,0:T(2,128)(2,1)S(1)}, bf16[2,512,2,128]{3,2,1,0:T(2,128)(2,1)}, u32[]{:S(2)}) copy-start(bf16[2,512,2,128]{3,2,1,0:T(2,128)(2,1)} %reshape_reshape.17) | copy-start | bytes 1572868
  43.2 3.4 %copy-start.6 = (bf16[16,64,2,128]{3,2,1,0:T(2,128)(2,1)S(1)}, bf16[16,64,2,128]{3,2,1,0:T(2,128)(2,1)}, u32[]{:S(2)}) copy-start(bf16[16,64,2,128]{3,2,1,0:T(2,128)(2,1)} %copy-done.5) | copy-start | bytes 1572868
  51.3 1.5 copy-start.14
  215.6 3.2 copy-start.10
  220.8 4.3 %copy-start.13 = (f32[256]{0:T(256)S(1)}, f32[256]{0:T(256)}, u32[]{:S(2)}) copy-start(f32[256]{0:T(256)} %param.19) | copy-start | bytes 3076
  223.4 1.7 copy-start.4
  240.1 2.7 copy-start.16
  242.1 0.8 copy-start.11
  275.5 4.5 %copy-start.17 = (s32[8]{0:T(128)S(1)}, s32[8]{0:T(128)}, u32[]{:S(2)}) copy-start(s32[8]{0:T(128)} %param.24) | copy-start | bytes 100
  278.1 9.8 %collective-permute-start = (bf16[256,2,2,128]{3,2,0,1:T(2,128)(2,1)S(1)}, bf16[256,2,2,128]{3,2,0,1:T(2,128)(2,1)S(1)}, u32[]{:S(2)}, u32[]{:S(2)}) collective-permute-start(bf16[256,2,2,128]{3,2,0,1:T(2,128)(2,1)S(1)} %slice.76), channel_id=1, source_target_pairs={{0,4},{4,8},{8,12},{12,16},{16,20},{20,24},{24,28},{28,32},{32,36}... | collective-permute-start | bytes 786440 | tf_op jit(solution)/shard_map/ppermute | solution.py:16
  321.2 2.1 copy-start.1
